TPU v7x, 512 devices: a whole 4x8x8 slice. The times are simulated.
512 devices in a mesh: grp: 16 (over z_lo, y), dev: 32 (over x, z_hi, core).
Axes of the slice: x: 4, y: 8, z: 8 (z_hi: 4, z_lo: 2; z = z_hi * 2 + z_lo), core: 2. Of those that a mesh axis runs over, the one named last changes fastest.
Arguments:
- sketch: bfloat16 [1048576, 256], P(('grp', 'dev')), may hold values from -4 to 4
- marginal_std: float32 [1048576], P(('grp', 'dev')), may hold values from 0.1 to 10
- cov_tiles: bfloat16 [9, 256, 256], replicated, may hold values from 0 to 1
- tile_cols: int32 [4096, 9], P(('grp', 'dev')), may hold values from -1 to 4095, as said below
Outputs:
- basis: float32 [1048576, 256], P(('grp', 'dev'))
- factor: float32 [256, 256], replicated
Inputs may be any that keep to these rules, and one draw needn't show every extreme that they name: `tile_cols`: tile t holds one line of 256 cells. The lines lie in depth order, except that the order within each aligned block of 4 tiles is permuted. Entry e of the list of tile t is the tile that holds the line e - 4 lines from the line of t (entry 4 is t itself), or -1 where that line lies beyond the ends of the field.
All inputs are finite; a program needn't handle non-finite values.
Results may differ from a plain program's by a relative error of at most 0.0035.
Values may be sent and summed in bfloat16 or wider, within the bound.
A program may use at most 64 MiB of HBM per device.

v0:
```python
import jax
import jax.numpy as jnp
from jax import lax
from jax.sharding import PartitionSpec as P


def with_halo(block, sides, width):
    for axis, dim in sides:
        count = lax.axis_size(axis)
        forward = [(i, i + 1) for i in range(count - 1)]
        backward = [(target, source) for source, target in forward]
        low = lax.ppermute(
            lax.slice_in_dim(block, block.shape[dim] - width, None, axis=dim), axis, forward
        )
        high = lax.ppermute(lax.slice_in_dim(block, 0, width, axis=dim), axis, backward)
        block = jnp.concatenate([low, block, high], axis=dim)
    return block


def per_device(sketch, marginal_std, cov_tiles, tile_cols):
    row_count, column_count = sketch.shape
    tile_size = cov_tiles.shape[1]
    row_tiles = row_count // tile_size
    scaled = (sketch.astype(jnp.float32) * marginal_std[:, None]).astype(jnp.bfloat16)
    extended = with_halo(scaled, ((("grp", "dev"), 0),), row_tiles * tile_size)
    extended_tiles = extended.reshape(-1, tile_size, column_count)
    first_tile = lax.axis_index(("grp", "dev")) * row_tiles
    present = tile_cols >= 0
    local_cols = jnp.where(present, tile_cols - first_tile + row_tiles, 0)
    gathered = extended_tiles[local_cols.T]
    gathered = jnp.where(present.T[:, :, None, None], gathered, jnp.zeros((), jnp.bfloat16))
    products = jnp.einsum("eij,etjk->tik", cov_tiles, gathered, preferred_element_type=jnp.float32)
    latent_field = products.reshape(row_count, column_count) * marginal_std[:, None]
    total_rows = row_count * lax.axis_size("grp") * lax.axis_size("dev")
    gram_matrix = (
        jnp.dot(latent_field.T, latent_field, precision=lax.Precision.HIGHEST) / total_rows
    )
    gram_matrix = lax.psum(gram_matrix, ("grp", "dev"))
    lower_factor = jnp.linalg.cholesky(gram_matrix)
    basis = lax.linalg.triangular_solve(
        lower_factor, latent_field, left_side=False, lower=True, transpose_a=True
    )
    return (basis, lower_factor.T)


def solution(mesh):
    in_specs = (P(("grp", "dev"), None), P(("grp", "dev")), P(), P(("grp", "dev"), None))
    out_specs = (P(("grp", "dev"), None), P())
    return jax.shard_map(
        per_device, mesh=mesh, in_specs=in_specs, out_specs=out_specs, check_vma=False
    )
```

profile of v0, /device:TPU:23, one launch (start us, length us, event | category | flops | bytes accessed | tf_op | source)
XLA Modules:
  0.0 430.0 jit_solution(10741237708848555990)
XLA Ops:
  7.2 1.6 multiply_convert_fusion
  8.9 6.4 %collective-permute-start = (bf16[2048,256]{1,0:T(8,128)(2,1)S(1)}, bf16[2048,256]{1,0:T(8,128)(2,1)S(1)}, u32[]{:S(2)}, u32[]{:S(2)}) collective-permute-start(bf16[2048,256]{1,0:T(8,128)(2,1)S(1)} %multiply_convert_fusion), channel_id=1, source_target_pairs={{0,1},{1,2},{2,3},{3,4},{4,5},{5,6},{6,7},{7,8},{8,9},{9,10},{10,1... | collective-permute-start | bytes 3145736 | tf_op jit(solution)/shard_map/ppermute | solution.py:12
  15.3 1.9 collective-permute-start.1
  17.6 15.5 %collective-permute-done = bf16[2048,256]{1,0:T(8,128)(2,1)S(1)} collective-permute-done((bf16[2048,256]{1,0:T(8,128)(2,1)S(1)}, bf16[2048,256]{1,0:T(8,128)(2,1)S(1)}, u32[]{:S(2)}, u32[]{:S(2)}) %collective-permute-start) | collective-permute-done | bytes 1048608 | tf_op jit(solution)/shard_map/ppermute | solution.py:12
  33.0 10.8 %collective-permute-done.1 = bf16[2048,256]{1,0:T(8,128)(2,1)} collective-permute-done((bf16[2048,256]{1,0:T(8,128)(2,1)S(1)}, bf16[2048,256]{1,0:T(8,128)(2,1)}, u32[]{:S(2)}, u32[]{:S(2)}) %collective-permute-start.1) | collective-permute-done | bytes 1048608 | tf_op jit(solution)/shard_map/ppermute | solution.py:15
  43.8 2.8 pad_maximum_fusion
  46.7 7.8 %gather_fusion = bf16[72,256,256]{2,1,0:T(8,128)(2,1)} fusion(bf16[24,256,256]{2,1,0:T(8,128)(2,1)} %bitcast.60, s32[1024]{0:T(1024)S(1)} %pad_clamp_fusion), kind=kCustom, calls=%fused_computation | custom fusion | bytes 18874656 | tf_op jit(solution)/shard_map/gather | solution.py:30
  54.5 5.5 %fusion = f32[8,256,256,1]{1,2,0,3:T(8,128)S(1)} fusion(bf16[9,8,256,256]{3,2,1,0:T(8,128)(2,1)} %bitcast.61, pred[9,8]{1,0:T(8,128)(4,1)S(1)} %copy.12, bf16[9,256,256]{2,1,0:T(8,128)(2,1)S(1)} %copy-done), kind=kOutput, calls=%fused_computation.3 | convolution fusion | flops 2420637696 | bytes 12714056 | tf_op jit(solution)/shard_map/eij,etjk->tik/dot_general | solution.py:32
  60.0 1.3 copy-done.1
  61.3 4.8 %fusion.7 = f32[256,256]{0,1:T(8,128)} fusion(f32[8,256,256,1]{1,2,0,3:T(8,128)S(1)} %fusion, f32[8,256]{1,0:T(8,128)S(1)} %mul.33), kind=kOutput, calls=%fused_computation.16 | convolution fusion | flops 1611202560 | bytes 2367488 | tf_op jit(solution)/shard_map/dot_general | solution.py:36
  66.1 1.9 bitcast_multiply_fusion
  68.0 273.6 %all-reduce.3.cloned.1.call-done = f32[256,256]{0,1:T(8,128)} async-done(((f32[256,256]{0,1:T(8,128)}), f32[256,256]{0,1:T(8,128)}) %all-reduce.3.cloned.1.call-update) | async-done | bytes 262160 | tf_op jit(solution)/shard_map/psum | solution.py:38
  344.4 11.7 %cholesky.50 = f32[128,128]{1,0:T(8,128)S(1)} custom-call(f32[128,128]{1,0:T(8,128)S(1)} %cholesky.118), custom_call_target="Cholesky" | custom-call | tf_op jit(solution)/shard_map/jit(cholesky)/cholesky | solution.py:39
  356.7 10.4 %custom-call.14 = f32[1,128,128]{1,2,0:T(8,128)} custom-call(f32[1,128,128]{2,1,0:T(8,128)S(1)} %get-tuple-element.29), custom_call_target="InvertDiagBlocksLowerTriangular" | custom-call | tf_op jit(solution)/shard_map/jit(cholesky)/cholesky | solution.py:39
  369.1 1.7 convolution_subtract_fusion.1
  370.9 13.4 %cholesky.105 = f32[128,128]{1,0:T(8,128)} custom-call(f32[128,128]{1,0:T(8,128)} %convolution_subtract_fusion.1), custom_call_target="Cholesky" | custom-call | tf_op jit(solution)/shard_map/jit(cholesky)/cholesky | solution.py:39
  387.2 1.7 fusion.13
  389.0 5.3 %while.1 = (s32[]{:T(128)}, f32[256,256]{1,0:T(8,128)S(1)}, s32[2,2]{1,0:T(2,128)S(1)}, f32[2,128,128]{2,1,0:T(8,128)}, s32[]{:T(128)}) while((s32[]{:T(128)}, f32[256,256]{1,0:T(8,128)S(1)}, s32[2,2]{1,0:T(2,128)S(1)}, f32[2,128,128]{2,1,0:T(8,128)}, s32[]{:T(128)}) %tuple.30), condition=%wide.while_cond, body=%wide.while_body.sunk | while | flops 2 | bytes 132705 | solution.py:40
  389.6 2.1 bitcast_dynamic-update-slice_fusion.2
  392.3 2.0 bitcast_dynamic-update-slice_fusion.2
  394.3 21.1 %custom-call.15 = f32[2,128,128]{1,2,0:T(8,128)} custom-call(f32[2,128,128]{2,1,0:T(8,128)} %get-tuple-element.9), custom_call_target="InvertDiagBlocksLowerTriangular" | custom-call | tf_op jit(solution)/shard_map/triangular_solve | solution.py:40
  415.4 1.9 fusion.8
  417.4 1.8 convolution_subtract_fusion
  420.5 1.8 copy.18
  (44 shorter events, 10.6 us)
Async XLA Ops:
  7.2 47.3 %copy-start = (bf16[9,256,256]{2,1,0:T(8,128)(2,1)S(1)}, bf16[9,256,256]{2,1,0:T(8,128)(2,1)}, u32[]{:S(2)}) copy-start(bf16[9,256,256]{2,1,0:T(8,128)(2,1)} %param.6) | copy-start | bytes 3538948
  7.2 10.0 %copy-start.7 = (f32[2048]{0:T(1024)S(1)}, f32[2048]{0:T(1024)}, u32[]{:S(2)}) copy-start(f32[2048]{0:T(1024)} %param.5) | copy-start | bytes 24580
  7.2 10.1 %copy-start.8 = (s32[8,9]{1,0:T(8,128)S(1)}, s32[8,9]{1,0:T(8,128)}, u32[]{:S(2)}) copy-start(s32[8,9]{1,0:T(8,128)} %param.7) | copy-start | bytes 868
  7.2 334.4 %all-reduce.3.cloned.1.call-start = ((), (), s32[]{:S(2)}) async-start(), calls=%async_computation | async-start | bytes 524288 | tf_op jit(solution)/shard_map/psum | solution.py:38
  8.9 24.1 %collective-permute-start = (bf16[2048,256]{1,0:T(8,128)(2,1)S(1)}, bf16[2048,256]{1,0:T(8,128)(2,1)S(1)}, u32[]{:S(2)}, u32[]{:S(2)}) collective-permute-start(bf16[2048,256]{1,0:T(8,128)(2,1)S(1)} %multiply_convert_fusion), channel_id=1, source_target_pairs={{0,1},{1,2},{2,3},{3,4},{4,5},{5,6},{6,7},{7,8},{8,9},{9,10},{10,1... | collective-permute-start | bytes 3145736 | tf_op jit(solution)/shard_map/ppermute | solution.py:12
  15.3 28.6 %collective-permute-start.1 = (bf16[2048,256]{1,0:T(8,128)(2,1)S(1)}, bf16[2048,256]{1,0:T(8,128)(2,1)}, u32[]{:S(2)}, u32[]{:S(2)}) collective-permute-start(bf16[2048,256]{1,0:T(8,128)(2,1)S(1)} %multiply_convert_fusion), channel_id=1, source_target_pairs={{1,0},{2,1},{3,2},{4,3},{5,4},{6,5},{7,6},{8,7},{9,8},{10,9},{11,1... | collective-permute-start | bytes 3145736 | tf_op jit(solution)/shard_map/ppermute | solution.py:15
  59.9 1.3 copy-start.1
  343.7 0.7 copy-start.4
  356.1 0.6 copy-start.5
  385.1 2.1 copy-start.2
  417.4 1.8 copy-start.6
  420.4 1.8 copy-start.3
Sparse Core Ops, SparseCore 0:
  66.2 275.3 all-reduce.2
where the time goes:
time: 431 us; the launch traced here: 430 us
  waiting for transfers between devices  300 us (70%)
  other arithmetic  67.5 us (16%)
  local copies, waits for them, and re-layouts  20.7 us (5%)
  matrix products  17.9 us (4%)
  between operations  15.6 us (4%)
  starting transfers between devices  8.33 us (2%)
    psum x1, waiting for transfers between devices, per_device(): gram_matrix = lax.psum(gram_matrix, ('grp', 'dev'))  274 us
    another operation x6, other arithmetic, per_device(): lower_factor = jnp.linalg.cholesky(gram_matrix)  37.2 us
    another operation x3, other arithmetic, per_device(): lax.linalg.triangular_solve(lower_factor, latent_field, left_side=False,...  21.2 us
    ppermute x1, waiting for transfers between devices, with_halo(): lax.ppermute(lax.slice_in_dim(block, block.shape[dim] - width, None, axis...  15.5 us
    ppermute x1, waiting for transfers between devices, with_halo(): lax.ppermute(lax.slice_in_dim(block, 0, width, axis=dim), axis, backward)  10.8 us
  transfers between devices with their start and end apart: 3, of which 3 were waited for; matrix products, arithmetic and copies ran while one was open for 1% of the time, Pallas kernels for 0%

commit v1 on v0

--- a/solution.py
+++ b/solution.py
@@ -35,7 +35,7 @@
     gram_matrix = (
         jnp.dot(latent_field.T, latent_field, precision=lax.Precision.HIGHEST) / total_rows
     )
-    gram_matrix = lax.psum(gram_matrix, ("grp", "dev"))
+    gram_matrix = jax.lax.psum(jax.lax.psum(gram_matrix, axis_name="dev"), axis_name="grp")
     lower_factor = jnp.linalg.cholesky(gram_matrix)
     basis = lax.linalg.triangular_solve(
         lower_factor, latent_field, left_side=False, lower=True, transpose_a=True

time: 431 us -> 593 us (1.38)
  the two profiles are of different devices: /device:TPU:23 before, /device:TPU:2 now
where the time goes in v1:
time: 593 us; the launch traced here: 592 us
  waiting for transfers between devices  458 us (77%)
  other arithmetic  67.3 us (11%)
  local copies, waits for them, and re-layouts  20.7 us (3%)
  matrix products  17.7 us (3%)
  between operations  15.6 us (3%)
  starting transfers between devices  12.5 us (2%)
    psum x1, waiting for transfers between devices, per_device(): jax.lax.psum(gram_matrix, axis_name='dev')  282 us
    psum x1, waiting for transfers between devices, per_device(): jax.lax.psum(jax.lax.psum(gram_matrix, axis_name='dev'), axis_name='grp')  153 us
    another operation x6, other arithmetic, per_device(): lower_factor = jnp.linalg.cholesky(gram_matrix)  37 us
    another operation x3, other arithmetic, per_device(): lax.linalg.triangular_solve(lower_factor, latent_field, left_side=False,...  21.2 us
    ppermute x1, waiting for transfers between devices, with_halo(): lax.ppermute(lax.slice_in_dim(block, 0, width, axis=dim), axis, backward)  13 us
  transfers between devices with their start and end apart: 4, of which 4 were waited for; matrix products, arithmetic and copies ran while one was open for 0% of the time, Pallas kernels for 0%

profile of v1, /device:TPU:2, one launch (start us, length us, event | category | flops | bytes accessed | tf_op | source)
XLA Modules:
  0.0 591.8 jit_solution(1049853280138594572)
XLA Ops:
  7.2 1.6 multiply_convert_fusion
  8.9 1.9 collective-permute-start
  10.8 10.3 %collective-permute-start.1 = (bf16[2048,256]{1,0:T(8,128)(2,1)S(1)}, bf16[2048,256]{1,0:T(8,128)(2,1)}, u32[]{:S(2)}, u32[]{:S(2)}) collective-permute-start(bf16[2048,256]{1,0:T(8,128)(2,1)S(1)} %multiply_convert_fusion), channel_id=1, source_target_pairs={{1,0},{2,1},{3,2},{4,3},{5,4},{6,5},{7,6},{8,7},{9,8},{10,9},{11,1... | collective-permute-start | bytes 3145736 | tf_op jit(solution)/shard_map/ppermute | solution.py:15
  21.5 10.3 %collective-permute-done = bf16[2048,256]{1,0:T(8,128)(2,1)S(1)} collective-permute-done((bf16[2048,256]{1,0:T(8,128)(2,1)S(1)}, bf16[2048,256]{1,0:T(8,128)(2,1)S(1)}, u32[]{:S(2)}, u32[]{:S(2)}) %collective-permute-start) | collective-permute-done | bytes 1048608 | tf_op jit(solution)/shard_map/ppermute | solution.py:12
  31.9 13.0 %collective-permute-done.1 = bf16[2048,256]{1,0:T(8,128)(2,1)} collective-permute-done((bf16[2048,256]{1,0:T(8,128)(2,1)S(1)}, bf16[2048,256]{1,0:T(8,128)(2,1)}, u32[]{:S(2)}, u32[]{:S(2)}) %collective-permute-start.1) | collective-permute-done | bytes 1048608 | tf_op jit(solution)/shard_map/ppermute | solution.py:15
  44.9 2.8 pad_maximum_fusion
  47.7 7.8 %gather_fusion = bf16[72,256,256]{2,1,0:T(8,128)(2,1)} fusion(bf16[24,256,256]{2,1,0:T(8,128)(2,1)} %bitcast.60, s32[1024]{0:T(1024)S(1)} %pad_clamp_fusion), kind=kCustom, calls=%fused_computation | custom fusion | bytes 18874656 | tf_op jit(solution)/shard_map/gather | solution.py:30
  55.5 5.3 fusion
  62.1 4.8 fusion.7
  67.2 281.9 %all-reduce.4.cloned.1.call-done = f32[256,256]{0,1:T(8,128)} async-done(((f32[256,256]{0,1:T(8,128)}), f32[256,256]{0,1:T(8,128)}) %all-reduce.4.cloned.1.call-update) | async-done | bytes 262160 | tf_op jit(solution)/shard_map/psum | solution.py:38
  349.2 1.9 bitcast_multiply_fusion
  351.1 152.6 %all-reduce.6.cloned.1.call-done = f32[256,256]{0,1:T(8,128)} async-done(((f32[256,256]{0,1:T(8,128)}), f32[256,256]{0,1:T(8,128)}) %all-reduce.6.cloned.1.call-update) | async-done | bytes 262160 | tf_op jit(solution)/shard_map/psum | solution.py:38
  506.5 11.7 %cholesky.50 = f32[128,128]{1,0:T(8,128)S(1)} custom-call(f32[128,128]{1,0:T(8,128)S(1)} %cholesky.118), custom_call_target="Cholesky" | custom-call | tf_op jit(solution)/shard_map/jit(cholesky)/cholesky | solution.py:39
  518.9 10.4 %custom-call.14 = f32[1,128,128]{1,2,0:T(8,128)} custom-call(f32[1,128,128]{2,1,0:T(8,128)S(1)} %get-tuple-element.29), custom_call_target="InvertDiagBlocksLowerTriangular" | custom-call | tf_op jit(solution)/shard_map/jit(cholesky)/cholesky | solution.py:39
  531.2 1.7 convolution_subtract_fusion.1
  533.0 13.2 %cholesky.105 = f32[128,128]{1,0:T(8,128)} custom-call(f32[128,128]{1,0:T(8,128)} %convolution_subtract_fusion.1), custom_call_target="Cholesky" | custom-call | tf_op jit(solution)/shard_map/jit(cholesky)/cholesky | solution.py:39
  549.1 1.7 fusion.13
  550.9 5.3 while.1
  551.5 2.1 bitcast_dynamic-update-slice_fusion.2
  554.1 2.1 bitcast_dynamic-update-slice_fusion.2
  556.2 21.1 %custom-call.15 = f32[2,128,128]{1,2,0:T(8,128)} custom-call(f32[2,128,128]{2,1,0:T(8,128)} %get-tuple-element.9), custom_call_target="InvertDiagBlocksLowerTriangular" | custom-call | tf_op jit(solution)/shard_map/triangular_solve | solution.py:40
  577.3 1.9 fusion.8
  579.2 1.8 convolution_subtract_fusion
  582.3 1.8 copy.18
  (47 shorter events, 12.2 us)
Async XLA Ops:
  7.2 48.3 %copy-start = (bf16[9,256,256]{2,1,0:T(8,128)(2,1)S(1)}, bf16[9,256,256]{2,1,0:T(8,128)(2,1)}, u32[]{:S(2)}) copy-start(bf16[9,256,256]{2,1,0:T(8,128)(2,1)} %param.6) | copy-start | bytes 3538948
  7.2 14.0 %copy-start.7 = (f32[2048]{0:T(1024)S(1)}, f32[2048]{0:T(1024)}, u32[]{:S(2)}) copy-start(f32[2048]{0:T(1024)} %param.5) | copy-start | bytes 24580
  7.2 14.0 %copy-start.8 = (s32[8,9]{1,0:T(8,128)S(1)}, s32[8,9]{1,0:T(8,128)}, u32[]{:S(2)}) copy-start(s32[8,9]{1,0:T(8,128)} %param.7) | copy-start | bytes 868
  7.2 341.9 %all-reduce.4.cloned.1.call-start = ((), (), s32[]{:S(2)}) async-start(), calls=%async_computation | async-start | bytes 524288 | tf_op jit(solution)/shard_map/psum | solution.py:38
  8.9 23.0 %collective-permute-start = (bf16[2048,256]{1,0:T(8,128)(2,1)S(1)}, bf16[2048,256]{1,0:T(8,128)(2,1)S(1)}, u32[]{:S(2)}, u32[]{:S(2)}) collective-permute-start(bf16[2048,256]{1,0:T(8,128)(2,1)S(1)} %multiply_convert_fusion), channel_id=1, source_target_pairs={{0,1},{1,2},{2,3},{3,4},{4,5},{5,6},{6,7},{7,8},{8,9},{9,10},{10,1... | collective-permute-start | bytes 3145736 | tf_op jit(solution)/shard_map/ppermute | solution.py:12
  10.8 34.0 %collective-permute-start.1 = (bf16[2048,256]{1,0:T(8,128)(2,1)S(1)}, bf16[2048,256]{1,0:T(8,128)(2,1)}, u32[]{:S(2)}, u32[]{:S(2)}) collective-permute-start(bf16[2048,256]{1,0:T(8,128)(2,1)S(1)} %multiply_convert_fusion), channel_id=1, source_target_pairs={{1,0},{2,1},{3,2},{4,3},{5,4},{6,5},{7,6},{8,7},{9,8},{10,9},{11,1... | collective-permute-start | bytes 3145736 | tf_op jit(solution)/shard_map/ppermute | solution.py:15
  60.8 1.3 copy-start.1
  67.0 436.8 %all-reduce.6.cloned.1.call-start = ((), (), s32[]{:S(2)}) async-start(), calls=%async_computation.1 | async-start | bytes 524288 | tf_op jit(solution)/shard_map/psum | solution.py:38
  505.8 0.7 copy-start.4
  518.2 0.6 copy-start.5
  547.0 2.1 copy-start.2
  579.2 1.8 copy-start.6
  582.3 1.8 copy-start.3
Sparse Core Ops, SparseCore 0:
  67.1 281.9 all-reduce.3
  352.0 151.6 all-reduce.5
